TPU v7x, 32 devices: a whole 2x2x4 slice. The times are simulated.
32 devices in a mesh: dp: 8 (over y, x, core), mp: 4 (over z).
Axes of the slice: x: 2, y: 2, z: 4, core: 2. Of those that a mesh axis runs over, the one named last changes fastest.
Arguments:
- activations: bfloat16 [16384, 1024], P('dp'), may hold values from -6 to 6
- cotangent: bfloat16 [16384, 1024], P('dp'), may hold values from -6 to 6
- level_table: bfloat16 [1024, 1024], P('dp'), may hold values from -6 to 6
- true_frames: int32 [16], P('dp'), may hold values from 4 to 16
- group_pattern: int32 [16], P('dp'), may hold values from 0 to 3
- noise_levels: int32 [4, 16], replicated, may hold values from 1 to 1023
- context_flags: int32 [16, 16], P('dp'), may hold values 0 or 1
- owner_list: int32 [288], replicated, may hold values from 0 to 287, as said below
- masters: float32 [4, 288, 128, 128], P('mp', 'dp')
- moment_one: float32 [4, 288, 128, 128], P('mp', 'dp')
- moment_two: float32 [4, 288, 128, 128], P('mp', 'dp')
- basis_left: float32 [4, 288, 128, 128], P('mp', 'dp'), as said below
- basis_right: float32 [4, 288, 128, 128], P('mp', 'dp'), as said below
Outputs:
- block_output: bfloat16 [16384, 1024], P('dp')
- input_grad: float32 [16384, 1024], P('dp')
- table_grad: float32 [1024, 1024], P(('dp', 'mp'))
- new_masters: float32 [4, 288, 128, 128], P('mp', 'dp')
- new_moment_one: float32 [4, 288, 128, 128], P('mp', 'dp')
- new_moment_two: float32 [4, 288, 128, 128], P('mp', 'dp')
- new_weights: bfloat16 [4, 288, 128, 128], P('mp', 'dp')
Inputs may be any that keep to these rules, and one draw needn't show every extreme that they name: `owner_list`: each tile number appears once; position p belongs to the dp index p // 36. `basis_left`: every tile is an orthogonal matrix. `basis_right`: every tile is an orthogonal matrix.
All inputs are finite; a program needn't handle non-finite values. No bound on the sum of `context_flags` on one device may be relied on, other than what follows from the above.
Results may differ from a plain program's by a relative error of at most 0.02.
Values may be sent and summed in bfloat16 or wider, within the bound.
A program may use at most 256 MiB of HBM per device.

v0:
```python
import jax
import jax.numpy as jnp
from jax import lax
from jax.sharding import PartitionSpec as P

D = 1024
H = 16
HD = 64
FF = 4096
FRAMES = 16
FRAME_TOK = 64
LEVELS = 1024
PATTERNS = 4
TILE = 128
HIGHEST = lax.Precision.HIGHEST
EPS_NORM = 1e-06
BETA_ONE = 0.5
BETA_TWO = 0.75
EPS_ADAM = 1e-08
DECAY = 0.01


def tile_layout(model_width, heads, head_dim, hidden, groups, tile_size):
    local_width = heads // groups * head_dim
    shapes = [
        (model_width, 3 * local_width),
        (local_width, model_width),
        (model_width, hidden // groups),
        (hidden // groups, model_width),
        (model_width, 6 * model_width // groups),
    ]
    counts = [height // tile_size * (breadth // tile_size) for height, breadth in shapes]
    return (shapes, counts)


def unpack(tile_stack, shapes, counts, tile_size):
    matrices = []
    offset = 0
    for (height, breadth), amount in zip(shapes, counts):
        stacked = tile_stack[offset : offset + amount].reshape(
            height // tile_size, breadth // tile_size, tile_size, tile_size
        )
        matrices.append(stacked.transpose(0, 2, 1, 3).reshape(height, breadth))
        offset = offset + amount
    return matrices


def pack(matrices, tile_size):
    stacked = []
    for matrix in matrices:
        height, breadth = matrix.shape
        stacked.append(
            matrix.reshape(height // tile_size, tile_size, breadth // tile_size, tile_size)
            .transpose(0, 2, 1, 3)
            .reshape(-1, tile_size, tile_size)
        )
    return jnp.concatenate(stacked, axis=0)


def kind_rates(tile_ids, counts):
    scales = [
        0.35 * D ** (-0.5),
        1.5 * (H * HD) ** (-0.5),
        0.5 * D ** (-0.5),
        0.5 * FF ** (-0.5),
        0.5 * D ** (-0.5),
    ]
    tile_rates = jnp.full(tile_ids.shape, scales[0], jnp.float32)
    boundary = 0
    for category in range(1, 5):
        boundary = boundary + counts[category - 1]
        tile_rates = jnp.where(tile_ids >= boundary, jnp.float32(scales[category]), tile_rates)
    return tile_rates


def layer_norm(stream):
    centered = stream - jnp.mean(stream, axis=-1, keepdims=True)
    inverse_std = lax.rsqrt(jnp.mean(centered * centered, axis=-1, keepdims=True) + EPS_NORM)
    return (centered * inverse_std, inverse_std)


def norm_back(grad_normed, normed, inverse_std):
    centered_grad = grad_normed - jnp.mean(grad_normed, axis=-1, keepdims=True)
    return inverse_std * (
        centered_grad - normed * jnp.mean(grad_normed * normed, axis=-1, keepdims=True)
    )


def gelu_tanh(values):
    return jax.nn.gelu(values, approximate=True)


def gelu_back(values, incoming):
    _, pullback = jax.vjp(gelu_tanh, values)
    return pullback(incoming)[0]


def contract_rows(left_side, right_side):
    return lax.dot_general(
        left_side, right_side, (((0,), (0,)), ((), ())), preferred_element_type=jnp.float32
    )


def contract_cols(left_side, right_side):
    return lax.dot_general(
        left_side, right_side, (((1,), (1,)), ((), ())), preferred_element_type=jnp.float32
    )


def block_scores(queries, key_all, mask_rows, score_scale):
    scores = (
        jnp.einsum("cqhd,ckhd->chqk", queries, key_all, preferred_element_type=jnp.float32)
        * score_scale
    )
    return jnp.where(mask_rows[:, None], scores, -1e30)


def attend_block(queries, key_all, value_all, mask_rows, score_scale):
    scores = block_scores(queries, key_all, mask_rows, score_scale)
    row_peak = jnp.max(scores, axis=-1, keepdims=True)
    exp_scores = jnp.exp(scores - row_peak)
    row_total = jnp.sum(exp_scores, axis=-1, keepdims=True)
    soft_rows = (exp_scores / row_total).astype(jnp.bfloat16)
    attended = jnp.einsum(
        "chqk,ckhd->cqhd", soft_rows, value_all, preferred_element_type=jnp.float32
    )
    return (attended, row_peak + jnp.log(row_total))


def attend_back(queries, key_all, value_all, mask_rows, log_total, grad_rows, score_scale):
    scores = block_scores(queries, key_all, mask_rows, score_scale)
    soft_rows = jnp.exp(scores - log_total)
    grad_soft = jnp.einsum(
        "cqhd,ckhd->chqk", grad_rows, value_all, preferred_element_type=jnp.float32
    )
    row_delta = jnp.sum(soft_rows * grad_soft, axis=-1, keepdims=True)
    grad_scores = (soft_rows * (grad_soft - row_delta)).astype(jnp.bfloat16)
    grad_query = (
        jnp.einsum("chqk,ckhd->cqhd", grad_scores, key_all, preferred_element_type=jnp.float32)
        * score_scale
    )
    grad_key = (
        jnp.einsum("chqk,cqhd->ckhd", grad_scores, queries, preferred_element_type=jnp.float32)
        * score_scale
    )
    grad_value = jnp.einsum(
        "chqk,cqhd->ckhd",
        soft_rows.astype(jnp.bfloat16),
        grad_rows,
        preferred_element_type=jnp.float32,
    )
    return (grad_query, grad_key, grad_value)


def body(
    activations,
    cotangent,
    level_table,
    true_frames,
    group_pattern,
    noise_levels,
    context_flags,
    owner_list,
    masters,
    moment_one,
    moment_two,
    basis_left,
    basis_right,
):
    groups = lax.axis_size("mp")
    member = lax.axis_index("mp")
    owner_rank = lax.axis_index("dp")
    shapes, counts = tile_layout(D, H, HD, FF, groups, TILE)
    slot_count = masters.shape[1]
    clip_count = true_frames.shape[0]
    frame_rows = clip_count * FRAMES
    tok_rows = activations.shape[0]
    clip_len = FRAMES * FRAME_TOK
    score_scale = HD ** (-0.5)
    inverse = jnp.argsort(owner_list)
    gathered, level_rows = (
        lax.all_gather(masters.astype(jnp.bfloat16), "dp", axis=1, tiled=True),
        lax.all_gather(level_table, "dp", axis=0, tiled=True),
    )
    w_qkv, w_out, w_up, w_down, w_mod = unpack(
        jnp.take(gathered[0], inverse, axis=0), shapes, counts, TILE
    )
    local_width = w_out.shape[0]
    heads_here = local_width // HD
    frame_index = jnp.arange(FRAMES, dtype=jnp.int32)
    valid_frame = frame_index[None, :] < true_frames[:, None]
    flagged = context_flags == 1
    in_context = flagged & valid_frame
    visible = valid_frame[:, None, :] & (
        jnp.logical_not(in_context)[:, :, None] | in_context[:, None, :]
    )
    pattern_hot = (group_pattern[:, None] == jnp.arange(PATTERNS, dtype=jnp.int32)[None, :]).astype(
        jnp.int32
    )
    pattern_levels = jnp.sum(pattern_hot[:, :, None] * noise_levels[None, :, :], axis=1)
    levels = jnp.where(flagged, 0, pattern_levels)
    level_hot = (
        levels.reshape(-1)[:, None] == jnp.arange(LEVELS, dtype=jnp.int32)[None, :]
    ).astype(jnp.bfloat16)
    embedded = jnp.dot(level_hot, level_rows, preferred_element_type=jnp.float32).astype(
        jnp.bfloat16
    )
    mod_part = jnp.dot(embedded, w_mod, preferred_element_type=jnp.float32)
    mod_all = lax.all_gather(mod_part, "mp", axis=1, tiled=True)
    modulation = (
        mod_all.reshape(frame_rows, groups, 6, D // groups)
        .transpose(0, 2, 1, 3)
        .reshape(frame_rows, 6, D)
    )
    token_mask = jnp.repeat(jnp.repeat(visible, FRAME_TOK, axis=1), FRAME_TOK, axis=2)
    stream = activations.astype(jnp.float32).reshape(frame_rows, FRAME_TOK, D)
    normed_one, inverse_one = layer_norm(stream)
    hidden_one = (
        (normed_one * (1.0 + modulation[:, 1, None, :]) + modulation[:, 0, None, :])
        .astype(jnp.bfloat16)
        .reshape(tok_rows, D)
    )
    qkv_rows = jnp.dot(hidden_one, w_qkv, preferred_element_type=jnp.float32).astype(jnp.bfloat16)
    queries = qkv_rows[:, :local_width].reshape(clip_count, clip_len, heads_here, HD)
    key_rows = qkv_rows[:, local_width : 2 * local_width].reshape(
        clip_count, clip_len, heads_here, HD
    )
    value_rows = qkv_rows[:, 2 * local_width :].reshape(clip_count, clip_len, heads_here, HD)
    block_rows = min(512, clip_len)
    block_total = clip_len // block_rows
    attended_parts = []
    log_parts = []
    for block_id in range(block_total):
        first_row = block_id * block_rows
        attended_blk, log_blk = attend_block(
            queries[:, first_row : first_row + block_rows],
            key_rows,
            value_rows,
            token_mask[:, first_row : first_row + block_rows],
            score_scale,
        )
        attended_parts.append(attended_blk)
        log_parts.append(log_blk)
    attended = (
        jnp.concatenate(attended_parts, axis=1).astype(jnp.bfloat16).reshape(tok_rows, local_width)
    )
    branch = (
        lax.psum(
            jnp.dot(attended, w_out, preferred_element_type=jnp.float32).astype(jnp.bfloat16), "mp"
        )
        .astype(jnp.float32)
        .reshape(frame_rows, FRAME_TOK, D)
    )
    middle = stream + modulation[:, 2, None, :] * branch
    normed_two, inverse_two = layer_norm(middle)
    hidden_two = (
        (normed_two * (1.0 + modulation[:, 4, None, :]) + modulation[:, 3, None, :])
        .astype(jnp.bfloat16)
        .reshape(tok_rows, D)
    )
    pre_act = jnp.dot(hidden_two, w_up, preferred_element_type=jnp.float32)
    activated = gelu_tanh(pre_act).astype(jnp.bfloat16)
    feed_out = (
        lax.psum(
            jnp.dot(activated, w_down, preferred_element_type=jnp.float32).astype(jnp.bfloat16),
            "mp",
        )
        .astype(jnp.float32)
        .reshape(frame_rows, FRAME_TOK, D)
    )
    result = middle + modulation[:, 5, None, :] * feed_out
    block_output = result.reshape(tok_rows, D).astype(jnp.bfloat16)
    regathered = lax.all_gather(masters.astype(jnp.bfloat16), "dp", axis=1, tiled=True)
    back_qkv, back_out, back_up, back_down, back_mod = unpack(
        jnp.take(regathered[0], inverse, axis=0), shapes, counts, TILE
    )
    grad_out = cotangent.astype(jnp.float32).reshape(frame_rows, FRAME_TOK, D)
    grad_feed = (modulation[:, 5, None, :] * grad_out).astype(jnp.bfloat16).reshape(tok_rows, D)
    grad_down = contract_rows(activated, grad_feed)
    grad_act = contract_cols(grad_feed, back_down).astype(jnp.bfloat16)
    grad_pre = gelu_back(pre_act, grad_act.astype(jnp.float32)).astype(jnp.bfloat16)
    grad_up = contract_rows(hidden_two, grad_pre)
    grad_gate_two = jnp.sum(grad_out * feed_out, axis=1)
    grad_hidden_two = (
        lax.psum(contract_cols(grad_pre, back_up).astype(jnp.bfloat16), "mp")
        .astype(jnp.float32)
        .reshape(frame_rows, FRAME_TOK, D)
    )
    grad_shift_two = jnp.sum(grad_hidden_two, axis=1)
    grad_scale_two = jnp.sum(grad_hidden_two * normed_two, axis=1)
    grad_middle = grad_out + norm_back(
        grad_hidden_two * (1.0 + modulation[:, 4, None, :]), normed_two, inverse_two
    )
    grad_gate_one = jnp.sum(grad_middle * branch, axis=1)
    grad_branch = (
        (modulation[:, 2, None, :] * grad_middle).astype(jnp.bfloat16).reshape(tok_rows, D)
    )
    grad_out_proj = contract_rows(attended, grad_branch)
    grad_attended = (
        contract_cols(grad_branch, back_out)
        .astype(jnp.bfloat16)
        .reshape(clip_count, clip_len, heads_here, HD)
    )
    query_parts = []
    grad_key = jnp.zeros((clip_count, clip_len, heads_here, HD), jnp.float32)
    grad_value = jnp.zeros((clip_count, clip_len, heads_here, HD), jnp.float32)
    for block_id in range(block_total):
        first_row = block_id * block_rows
        grad_query_blk, grad_key_blk, grad_value_blk = attend_back(
            queries[:, first_row : first_row + block_rows],
            key_rows,
            value_rows,
            token_mask[:, first_row : first_row + block_rows],
            log_parts[block_id],
            grad_attended[:, first_row : first_row + block_rows],
            score_scale,
        )
        query_parts.append(grad_query_blk)
        grad_key = grad_key + grad_key_blk
        grad_value = grad_value + grad_value_blk
    grad_query = jnp.concatenate(query_parts, axis=1)
    grad_qkv = jnp.concatenate(
        [
            grad_query.astype(jnp.bfloat16).reshape(tok_rows, local_width),
            grad_key.astype(jnp.bfloat16).reshape(tok_rows, local_width),
            grad_value.astype(jnp.bfloat16).reshape(tok_rows, local_width),
        ],
        axis=1,
    )
    grad_w_qkv = contract_rows(hidden_one, grad_qkv)
    grad_hidden_one = (
        lax.psum(contract_cols(grad_qkv, back_qkv).astype(jnp.bfloat16), "mp")
        .astype(jnp.float32)
        .reshape(frame_rows, FRAME_TOK, D)
    )
    grad_shift_one = jnp.sum(grad_hidden_one, axis=1)
    grad_scale_one = jnp.sum(grad_hidden_one * normed_one, axis=1)
    input_grad = (
        grad_middle
        + norm_back(grad_hidden_one * (1.0 + modulation[:, 1, None, :]), normed_one, inverse_one)
    ).reshape(tok_rows, D)
    grad_mod = jnp.stack(
        [
            grad_shift_one,
            grad_scale_one,
            grad_gate_one,
            grad_shift_two,
            grad_scale_two,
            grad_gate_two,
        ],
        axis=1,
    )
    grad_mod_own = lax.dynamic_index_in_dim(
        grad_mod.reshape(frame_rows, 6, groups, D // groups), member, axis=2, keepdims=False
    )
    grad_mod_own = grad_mod_own.reshape(frame_rows, 6 * D // groups).astype(jnp.bfloat16)
    grad_w_mod = contract_rows(embedded, grad_mod_own)
    grad_embedded = contract_cols(grad_mod_own, back_mod)
    table_term = lax.dot_general(
        level_hot.astype(jnp.float32),
        grad_embedded,
        (((0,), (0,)), ((), ())),
        precision=HIGHEST,
        preferred_element_type=jnp.float32,
    )
    table_grad = lax.psum_scatter(table_term, ("dp", "mp"), scatter_dimension=0, tiled=True)
    packed = pack([grad_w_qkv, grad_out_proj, grad_up, grad_down, grad_w_mod], TILE)
    owned = jnp.take(packed, owner_list, axis=0)
    reduced = lax.psum_scatter(
        owned[None].astype(jnp.bfloat16), "dp", scatter_dimension=1, tiled=True
    ).astype(jnp.float32)[0]
    tile_ids = lax.dynamic_slice_in_dim(owner_list, owner_rank * slot_count, slot_count)
    rotated = jnp.einsum("pji,pjk->pik", basis_left[0], reduced, precision=HIGHEST)
    rotated = jnp.einsum("pik,pkl->pil", rotated, basis_right[0], precision=HIGHEST)
    new_one = BETA_ONE * moment_one[0] + (1.0 - BETA_ONE) * rotated
    new_two = BETA_TWO * moment_two[0] + (1.0 - BETA_TWO) * rotated * rotated
    direction = new_one / (jnp.sqrt(new_two) + EPS_ADAM)
    turned = jnp.einsum("pij,pjk->pik", basis_left[0], direction, precision=HIGHEST)
    turned = jnp.einsum("pik,plk->pil", turned, basis_right[0], precision=HIGHEST)
    tile_rates = kind_rates(tile_ids, counts)
    new_masters = masters[0] - tile_rates[:, None, None] * (turned + DECAY * masters[0])
    return (
        block_output,
        input_grad,
        table_grad,
        new_masters[None],
        new_one[None],
        new_two[None],
        new_masters[None].astype(jnp.bfloat16),
    )


def solution(mesh):
    in_specs = (
        P("dp", None),
        P("dp", None),
        P("dp", None),
        P("dp"),
        P("dp"),
        P(),
        P("dp", None),
        P(),
        P("mp", "dp", None, None),
        P("mp", "dp", None, None),
        P("mp", "dp", None, None),
        P("mp", "dp", None, None),
        P("mp", "dp", None, None),
    )
    out_specs = (
        P("dp", None),
        P("dp", None),
        P(("dp", "mp"), None),
        P("mp", "dp", None, None),
        P("mp", "dp", None, None),
        P("mp", "dp", None, None),
        P("mp", "dp", None, None),
    )
    return jax.shard_map(body, mesh=mesh, in_specs=in_specs, out_specs=out_specs, check_vma=False)
```

profile of v0, /device:TPU:0, one launch (start us, length us, event | category | flops | bytes accessed | tf_op | source)
XLA Modules:
  0.0 1286.3 jit_solution(2902918120802603525)
XLA Ops:
  32.7 8.9 all-gather.3.cloned.1.call-done
  43.8 59.1 %all-gather.5.cloned.1.call-done = bf16[1,288,128,128]{3,2,0,1:T(8,128)(2,1)} async-done(((bf16[1,36,128,128]{3,2,0,1:T(8,128)(2,1)}), bf16[1,288,128,128]{3,2,0,1:T(8,128)(2,1)}) %all-gather.5.cloned.1.call-update) | async-done | bytes 9437200 | tf_op jit(solution)/shard_map/all_gather | solution.py:182
  102.8 14.0 %gather_fusion.1 = bf16[288,128,128]{2,1,0:T(8,128)(2,1)} fusion(bf16[288,128,128]{2,1,0:T(8,128)(2,1)} %bitcast.414, s32[1024]{0:T(1024)S(1)} %pad_clamp_fusion.1), kind=kCustom, calls=%fused_computation.clone | custom fusion | bytes 18875520 | tf_op jit(solution)/shard_map/jit(_take)/gather | solution.py:186
  116.8 8.2 broadcast_select_fusion
  127.9 4.0 slice.97
  135.7 4.9 copy.189
  143.5 20.2 %all_gather.12 = f32[32,6144]{1,0:T(8,128)} all-gather(f32[32,1536]{1,0:T(8,128)S(1)} %fusion.68), channel_id=1, replica_groups=mesh['dp'=8,'mp'=4] {'mp'}, dimensions={1}, use_global_device_ids=true | all-gather | bytes 983040 | tf_op jit(solution)/shard_map/all_gather | solution.py:209
  182.1 4.7 reshape.481
  194.9 4.4 reshape.480
  199.4 4.0 copy.198
  203.4 4.6 fusion.155
  217.9 3.9 fusion.156
  247.6 6.3 convolution_convert_fusion.2
  253.9 137.4 %all-reduce.5.cloned.1.call-done = bf16[2048,1024]{1,0:T(8,128)(2,1)} async-done(((bf16[2048,1024]{1,0:T(8,128)(2,1)}), bf16[2048,1024]{1,0:T(8,128)(2,1)}) %all-reduce.5.cloned.1.call-update) | async-done | bytes 4194320 | tf_op jit(solution)/shard_map/psum | solution.py:248
  391.3 5.0 fusion.70
  401.8 14.3 %fusion.40 = (bf16[1024,2048]{1,0:T(8,128)(2,1)}, bf16[1024,2048]{1,0:T(8,128)(2,1)}, f32[2048,1024]{0,1:T(8,128)S(1)}) fusion(bf16[2048,1024]{0,1:T(8,128)(2,1)} %convolution_convert_fusion.2, bf16[2048,1024]{1,0:T(8,128)(2,1)S(1)} %fusion.35, bf16[128,8,8,128]{3,2,1,0:T(8,128)(2,1)S(1)} %bitcast.439), kind=kOutput, calls=%fused_computation.70 | convolution fusion | flops 4343201792 | bytes 27262976 | tf_op jit(solution)/shard_map/dot_general | solution.py:261
  419.5 12.9 %fusion.63 = bf16[2048,1024]{1,0:T(8,128)(2,1)} fusion(f32[2048,1024]{0,1:T(8,128)S(1)} %get-tuple-element.58, bf16[2048,1024]{0,1:T(8,128)(2,1)} %convolution_convert_fusion.2, bf16[128,8,8,128]{3,2,1,0:T(8,128)(2,1)S(1)} %bitcast.440), kind=kOutput, calls=%fused_computation.107 | convolution fusion | flops 4341104640 | bytes 18874368 | tf_op jit(solution)/shard_map/dot_general | solution.py:105
  433.8 12.7 fusion.62
  446.5 140.1 %all-reduce.7.cloned.1.call-done = bf16[2048,1024]{1,0:T(8,128)(2,1)} async-done(((bf16[2048,1024]{1,0:T(8,128)(2,1)}), bf16[2048,1024]{1,0:T(8,128)(2,1)}) %all-reduce.7.cloned.1.call-update) | async-done | bytes 4194320 | tf_op jit(solution)/shard_map/psum | solution.py:285
  586.6 7.9 fusion.54
  594.9 8.3 fusion.28
  607.5 4.4 reshape.483
  616.5 14.2 %multiply_reduce_fusion.1 = (f32[2,4,512]{2,1,0:T(4,128)S(1)}, f32[2,4,512,1024]{3,2,1,0:T(8,128)}) fusion(f32[2,4,512,1024]{3,2,1,0:T(8,128)} %copy-done.5, f32[2,4,512]{2,1,0:T(4,128)} %bitcast.454, bf16[2,512,4,64]{1,3,2,0:T(8,128)(2,1)} %copy.253, bf16[2,1024,4,64]{1,3,2,0:T(8,128)(2,1)} %copy.198), kind=kOutput, calls=%fused_computation.8 | convolution fusion | flops 549449728 | bytes 35160064 | tf_op jit(solution)/shard_map/cqhd,ckhd->chqk/dot_general | solution.py:133
  633.4 10.3 multiply_convert_fusion.1
  643.8 7.3 fusion.114
  655.3 7.6 fusion.36
  663.0 13.7 %multiply_reduce_fusion = (f32[2,4,512]{2,1,0:T(4,128)S(1)}, f32[2,4,512,1024]{3,2,1,0:T(8,128)}) fusion(f32[2,4,512,1024]{3,2,1,0:T(8,128)} %copy-done.4, f32[2,4,512]{2,1,0:T(4,128)S(1)} %bitcast.452, bf16[2,512,4,64]{1,3,2,0:T(8,128)(2,1)S(1)} %copy-done.30, bf16[2,1024,4,64]{1,3,2,0:T(8,128)(2,1)S(1)} %copy-done.21), kind=kOutput, calls=%fused_computation.5 | convolution fusion | flops 549449728 | bytes 35160064 | tf_op jit(solution)/shard_map/cqhd,ckhd->chqk/dot_general | solution.py:133
  676.6 9.2 fusion.106
  688.3 10.7 multiply_convert_fusion
  699.0 6.2 fusion.113
  711.6 5.2 convolution_convert_fusion.1
  719.5 6.9 copy.240
  726.4 6.5 copy.237
  734.2 6.5 copy.239
  740.7 8.7 fusion.161
  749.5 5.7 fusion.160
  756.6 6.5 copy.238
  763.1 6.4 fusion.158
  776.0 230.9 %all-reduce.9.cloned.1.call-done = (bf16[2048,1024]{1,0:T(8,128)(2,1)}, bf16[2048,1024]{1,0:T(8,128)(2,1)}) async-done(((bf16[2048,1024]{1,0:T(8,128)(2,1)}, bf16[2048,1024]{1,0:T(8,128)(2,1)}), (bf16[2048,1024]{1,0:T(8,128)(2,1)}, bf16[2048,1024]{1,0:T(8,128)(2,1)})) %all-reduce.9.cloned.1.call-update) | async-done | bytes 8388624 | tf_op jit(solution)/shard_map/psum | solution.py:264
  1006.8 17.0 %fusion.49 = (bf16[32,1024]{1,0:T(8,128)(2,1)S(1)}, bf16[32,1024]{1,0:T(8,128)(2,1)S(1)}, bf16[32,1024]{1,0:T(8,128)(2,1)S(1)}, bf16[32,1024]{1,0:T(8,128)(2,1)S...) fusion(bf16[2048,1024]{1,0:T(8,128)(2,1)} %all-reduce.7.cloned.1.call-done, ...), kind=kLoop, calls=%fused_computation.83 | loop fusion | flops 58523648 | bytes 25870336 | tf_op jit(solution)/shard_map/reduce_sum | solution.py:290
  1027.8 14.0 %gather_fusion = bf16[288,128,128]{2,1,0:T(8,128)(2,1)} fusion(bf16[288,128,128]{2,1,0:T(8,128)(2,1)} %constant_dynamic-update-slice_fusion.9, s32[1024]{0:T(1024)S(1)} %copy-done.78), kind=kCustom, calls=%fused_computation.1 | custom fusion | bytes 18875520 | tf_op jit(solution)/shard_map/jit(_take)/gather | solution.py:368
  1041.8 9.3 fusion
  1058.6 8.1 fusion.43
  1067.1 12.4 fusion.46
  1079.5 47.6 %reduce-scatter.5.cloned.1.call-done = bf16[1,36,128,128]{3,2,1,0:T(8,128)(2,1)} async-done(((bf16[1,288,128,128]{3,2,1,0:T(8,128)(2,1)}), bf16[1,36,128,128]{3,2,1,0:T(8,128)(2,1)}) %reduce-scatter.5.cloned.1.call-update) | async-done | bytes 1179664 | tf_op jit(solution)/shard_map/reduce_scatter | solution.py:369
  1130.6 4.4 fusion.76
  1138.8 5.1 bitcast_subtract_fusion
  1149.4 129.7 %reduce-scatter.3.cloned.1.call-done = f32[32,1024]{1,0:T(8,128)} async-done(((f32[1024,1024]{1,0:T(8,128)}), f32[32,1024]{1,0:T(8,128)}) %reduce-scatter.3.cloned.1.call-update) | async-done | bytes 131088 | tf_op jit(solution)/shard_map/reduce_scatter | solution.py:366
  (317 shorter events, 170.4 us)
Async XLA Ops:
  7.2 1119.9 %copy-start = (f32[1,36,128,128]{3,2,1,0:T(8,128)S(1)}, f32[1,36,128,128]{3,2,1,0:T(8,128)}, u32[]{:S(2)}) copy-start(f32[1,36,128,128]{3,2,1,0:T(8,128)} %param.26) | copy-start | bytes 7077892
  7.2 15.9 %copy-start.76 = (s32[288]{0:T(512)S(1)}, s32[288]{0:T(512)}, u32[]{:S(2)}) copy-start(s32[288]{0:T(512)} %param.22) | copy-start | bytes 3460
  7.2 34.5 %all-gather.3.cloned.1.call-start = ((), (), s32[]{:S(2)}) async-start(), calls=%async_computation.2 | async-start | bytes 2359296 | tf_op jit(solution)/shard_map/all_gather | solution.py:183
  7.9 94.9 %all-gather.5.cloned.1.call-start = ((), (), s32[]{:S(2)}) async-start(), calls=%async_computation.3 | async-start | bytes 10616832 | tf_op jit(solution)/shard_map/all_gather | solution.py:182
  10.9 380.4 %all-reduce.5.cloned.1.call-start = ((), (), s32[]{:S(2)}) async-start(), calls=%async_computation.4 | async-start | bytes 8388608 | tf_op jit(solution)/shard_map/psum | solution.py:248
  13.2 28.5 %copy-start.79 = (s32[32]{0:T(128)}, s32[32]{0:T(128)S(1)}, u32[]{:S(2)}) copy-start(s32[32]{0:T(128)S(1)} %eq.43) | copy-start | bytes 388
  29.7 139.1 %copy-start.56 = (f32[2048]{0:T(1024)}, f32[2048]{0:T(1024)S(1)}, u32[]{:S(2)}) copy-start(f32[2048]{0:T(1024)S(1)} %broadcast_multiply_fusion.5) | copy-start | bytes 24580
  32.7 136.1 %copy-start.62 = (f32[2048]{0:T(1024)}, f32[2048]{0:T(1024)S(1)}, u32[]{:S(2)}) copy-start(f32[2048]{0:T(1024)S(1)} %add_rsqrt_fusion.1) | copy-start | bytes 24580
  43.7 96.9 %copy-start.52 = (bf16[32,1024]{1,0:T(8,128)(2,1)}, bf16[32,1024]{1,0:T(8,128)(2,1)S(1)}, u32[]{:S(2)}) copy-start(bf16[32,1024]{1,0:T(8,128)(2,1)S(1)} %convolution_convert_fusion.5) | copy-start | bytes 196612
  182.1 35.7 %copy-start.13 = (bf16[2,1024,4,64]{1,3,2,0:T(8,128)(2,1)}, bf16[2,1024,4,64]{1,3,2,0:T(8,128)(2,1)S(1)}, u32[]{:S(2)}) copy-start(bf16[2,1024,4,64]{1,3,2,0:T(8,128)(2,1)S(1)} %copy.197) | copy-start | bytes 3145732
  237.3 349.3 %all-reduce.7.cloned.1.call-start = ((), (), s32[]{:S(2)}) async-start(), calls=%async_computation.5 | async-start | bytes 8388608 | tf_op jit(solution)/shard_map/psum | solution.py:285
  391.3 8.1 copy-start.36
  391.3 8.1 copy-start.54
  401.8 14.3 %copy-start.18 = (bf16[2048,1024]{1,0:T(8,128)(2,1)}, bf16[2048,1024]{1,0:T(8,128)(2,1)S(1)}, u32[]{:S(2)}) copy-start(bf16[2048,1024]{1,0:T(8,128)(2,1)S(1)} %fusion.35) | copy-start | bytes 12582916
  419.5 13.0 %copy-start.65 = (f32[2,4,512]{2,1,0:T(4,128)S(1)}, f32[2,4,512]{2,1,0:T(4,128)}, u32[]{:S(2)}) copy-start(f32[2,4,512]{2,1,0:T(4,128)} %copy-done.64) | copy-start | bytes 49156
  419.5 13.0 %copy-start.75 = (f32[2,4,512]{2,1,0:T(4,128)S(1)}, f32[2,4,512]{2,1,0:T(4,128)}, u32[]{:S(2)}) copy-start(f32[2,4,512]{2,1,0:T(4,128)} %copy-done.74) | copy-start | bytes 49156
  419.5 13.6 %copy-start.67 = (f32[2,4,512]{2,1,0:T(4,128)S(1)}, f32[2,4,512]{2,1,0:T(4,128)}, u32[]{:S(2)}) copy-start(f32[2,4,512]{2,1,0:T(4,128)} %copy-done.66) | copy-start | bytes 49156
  432.5 574.3 %all-reduce.9.cloned.1.call-start = ((), (), s32[]{:S(2)}) async-start(), calls=%async_computation.8 | async-start | bytes 16777216 | tf_op jit(solution)/shard_map/psum | solution.py:264
  586.6 8.3 copy-start.11
  594.5 8.8 copy-start.68
  594.5 8.8 copy-start.70
  616.5 14.2 %slice-start.4 = ((s8[16777216]{0:T(1024)(128)(4,1)}), s8[4194304]{0:T(1024)(128)(4,1)S(1)}, s32[]{:S(2)}) async-start(s8[16777216]{0:T(1024)(128)(4,1)} %bitcast.403), calls=%async_computation.13 | async-start | bytes 8388608
  616.5 14.2 %slice-start.5 = ((s8[16777216]{0:T(1024)(128)(4,1)}), s8[4194304]{0:T(1024)(128)(4,1)S(1)}, s32[]{:S(2)}) async-start(s8[16777216]{0:T(1024)(128)(4,1)} %bitcast.403), calls=%async_computation.14 | async-start | bytes 8388608
  616.5 15.7 %slice-start.6 = ((s8[16777216]{0:T(1024)(128)(4,1)}), s8[4194304]{0:T(1024)(128)(4,1)S(1)}, s32[]{:S(2)}) async-start(s8[16777216]{0:T(1024)(128)(4,1)} %bitcast.403), calls=%async_computation.15 | async-start | bytes 8388608
  616.5 16.9 %slice-start.7 = ((s8[16777216]{0:T(1024)(128)(4,1)}), s8[4194304]{0:T(1024)(128)(4,1)S(1)}, s32[]{:S(2)}) async-start(s8[16777216]{0:T(1024)(128)(4,1)} %bitcast.403), calls=%async_computation.16 | async-start | bytes 8388608
  616.5 16.9 %copy-start.59 = (f32[1,8,512]{2,1,0:T(8,128)S(1)}, f32[1,8,512]{2,1,0:T(8,128)}, u32[]{:S(2)}) copy-start(f32[1,8,512]{2,1,0:T(8,128)} %log_add_fusion.1) | copy-start | bytes 49156
  662.9 13.7 %copy-start.60 = (f32[1,8,512]{2,1,0:T(8,128)S(1)}, f32[1,8,512]{2,1,0:T(8,128)}, u32[]{:S(2)}) copy-start(f32[1,8,512]{2,1,0:T(8,128)} %log_add_fusion.1) | copy-start | bytes 49156
  662.9 25.3 %slice-start = ((s8[16777216]{0:T(1024)(128)(4,1)}), s8[4194304]{0:T(1024)(128)(4,1)S(1)}, s32[]{:S(2)}) async-start(s8[16777216]{0:T(1024)(128)(4,1)} %bitcast.401), calls=%async_computation.9 | async-start | bytes 8388608
  662.9 25.3 %slice-start.1 = ((s8[16777216]{0:T(1024)(128)(4,1)}), s8[4194304]{0:T(1024)(128)(4,1)S(1)}, s32[]{:S(2)}) async-start(s8[16777216]{0:T(1024)(128)(4,1)} %bitcast.401), calls=%async_computation.10 | async-start | bytes 8388608
  663.0 25.3 %slice-start.2 = ((s8[16777216]{0:T(1024)(128)(4,1)}), s8[4194304]{0:T(1024)(128)(4,1)S(1)}, s32[]{:S(2)}) async-start(s8[16777216]{0:T(1024)(128)(4,1)} %bitcast.401), calls=%async_computation.11 | async-start | bytes 8388608
  676.6 11.6 slice-start.3
  688.2 10.7 copy-start.14
  688.3 16.9 %copy-start.15 = (f32[2,4,64,1024]{3,2,1,0:T(8,128)S(1)}, f32[2,4,64,1024]{3,2,1,0:T(8,128)}, u32[]{:S(2)}) copy-start(f32[2,4,64,1024]{3,2,1,0:T(8,128)} %fusion.157) | copy-start | bytes 6291460
  716.8 410.2 %reduce-scatter.5.cloned.1.call-start = ((), (), s32[]{:S(2)}) async-start(), calls=%async_computation.7 | async-start | bytes 10616832 | tf_op jit(solution)/shard_map/reduce_scatter | solution.py:369
  740.7 8.8 copy-start.33
  740.7 8.8 copy-start.82
  770.8 236.0 %copy-start.37 = (f32[32,1024]{1,0:T(8,128)S(1)}, f32[32,1024]{1,0:T(8,128)}, u32[]{:S(2)}) copy-start(f32[32,1024]{1,0:T(8,128)} %get-tuple-element.43) | copy-start | bytes 393220
  770.8 236.0 %copy-start.72 = (f32[32,64]{1,0:T(8,128)S(1)}, f32[32,64]{1,0:T(8,128)}, u32[]{:S(2)}) copy-start(f32[32,64]{1,0:T(8,128)} %rsqrt.27) | copy-start | bytes 24580
  770.8 236.0 %copy-start.73 = (f32[32,64]{1,0:T(8,128)S(1)}, f32[32,64]{1,0:T(8,128)}, u32[]{:S(2)}) copy-start(f32[32,64]{1,0:T(8,128)} %div.65) | copy-start | bytes 24580
  1006.8 17.8 %copy-start.61 = (bf16[4,8,8,128]{3,2,1,0:T(8,128)(2,1)S(1)}, bf16[4,8,8,128]{3,2,1,0:T(8,128)(2,1)}, u32[]{:S(2)}) copy-start(bf16[4,8,8,128]{3,2,1,0:T(8,128)(2,1)} %copy.266) | copy-start | bytes 196612
  1027.8 14.0 %copy-start.81 = (pred[288]{0:T(512)(128)(4,1)S(1)}, pred[288]{0:T(512)(128)(4,1)}, u32[]{:S(2)}) copy-start(pred[288]{0:T(512)(128)(4,1)} %compare_and_fusion.1) | copy-start | bytes 868
  1051.1 228.0 %reduce-scatter.3.cloned.1.call-start = ((), (), s32[]{:S(2)}) async-start(), calls=%async_computation.6 | async-start | bytes 4325376 | tf_op jit(solution)/shard_map/reduce_scatter | solution.py:366
  1053.7 13.0 %copy-start.51 = (f32[32,1024]{1,0:T(8,128)S(1)}, f32[32,1024]{1,0:T(8,128)}, u32[]{:S(2)}) copy-start(f32[32,1024]{1,0:T(8,128)} %get-tuple-element.45) | copy-start | bytes 393220
  1057.6 9.1 copy-start.3
  1057.6 9.5 copy-start.8
  1127.1 8.0 copy-start.39
  1130.6 8.2 copy-start.22
  1130.6 8.2 copy-start.23
  (52 other events, 247.6 us)
Sparse Core Ops, SparseCore 0:
  9.9 31.7 all-gather.2
  44.1 58.6 all-gather.4
  237.4 153.8 all-reduce.4
  432.6 153.9 all-reduce.6
  717.0 289.8 all-reduce.8
  1051.2 75.7 reduce-scatter.4
  1129.9 149.1 reduce-scatter.2
where the time goes:
time: 1300 us; the launch traced here: 1290 us
  waiting for transfers between devices  754 us (58%)
  matrix products  191 us (15%)
  local copies, waits for them, and re-layouts  168 us (13%)
  other arithmetic  137 us (11%)
  blocking collectives  20.2 us (2%)
  between operations  15.8 us (1%)
    psum x1, waiting for transfers between devices, body(): lax.psum(jnp.dot(activated, w_down, preferred_element_type=jnp.float32).a...  231 us
    psum x1, waiting for transfers between devices, body(): lax.psum(contract_cols(grad_pre, back_up).astype(jnp.bfloat16), 'mp')  140 us
    psum x1, waiting for transfers between devices, body(): lax.psum(jnp.dot(attended, w_out, preferred_element_type=jnp.float32).ast...  137 us
    reduce_scatter x1, waiting for transfers between devices, body(): lax.psum_scatter(table_term, ('dp', 'mp'), scatter_dimension=0, tiled=True)  130 us
    all_gather x1, waiting for transfers between devices, body(): lax.all_gather(masters.astype(jnp.bfloat16), 'dp', axis=1, tiled=True)  59.1 us
    reduce_scatter x1, waiting for transfers between devices, body(): lax.psum_scatter(owned[None].astype(jnp.bfloat16), 'dp', scatter_dimensio...  47.6 us
    unnamed x205, local copies, waits for them, and re-layouts  36.9 us
    dot_general x5, matrix products, contract_cols(): lax.dot_general(left_side, right_side, (((1,), (1,)), ((), ())), preferre...  29.2 us
  transfers between devices with their start and end apart: 7, of which 7 were waited for; matrix products, arithmetic and copies ran while one was open for 13% of the time, Pallas kernels for 0%

commit v1 on v0

--- a/solution.py
+++ b/solution.py
@@ -1,3 +1,4 @@
+import functools
 import jax
 import jax.numpy as jnp
 from jax import lax
@@ -18,6 +19,28 @@
 BETA_TWO = 0.75
 EPS_ADAM = 1e-08
 DECAY = 0.01
+
+
+def advance_the_cube(frame, mesh_dim):
+    f_next = lax.axis_size(mesh_dim)
+    local_now = lax.axis_index(mesh_dim)
+    front, y_new, w1 = (f_next, local_now, frame.shape[1])
+    all_rows = tuple(((jj, (jj + 1) % front) for jj in range(front)))
+    v_now = jnp.zeros((*frame.shape[:1], front * w1, *frame.shape[2:]), frame.dtype)
+    v_now = lax.dynamic_update_slice_in_dim(v_now, frame, y_new * w1, axis=1)
+    far_arr = r_now = frame
+    fields = tuple(((jj, (jj - 1) % front) for jj in range(front)))
+    low = front // 2
+    for i in range(1, low + 1):
+        far_arr = lax.ppermute(far_arr, perm=all_rows, axis_name=mesh_dim)
+        v_now = lax.dynamic_update_slice_in_dim(v_now, far_arr, (y_new - i) % front * w1, axis=1)
+        if i < front - low:
+            r_now = lax.ppermute(r_now, mesh_dim, perm=fields)
+            v_now = lax.dynamic_update_slice_in_dim(v_now, r_now, (y_new + i) % front * w1, axis=1)
+    return v_now
+
+
+prepare_shards_up = functools.partial(advance_the_cube, mesh_dim="dp")
 
 
 def tile_layout(model_width, heads, head_dim, hidden, groups, tile_size):
@@ -179,7 +202,7 @@
     score_scale = HD ** (-0.5)
     inverse = jnp.argsort(owner_list)
     gathered, level_rows = (
-        lax.all_gather(masters.astype(jnp.bfloat16), "dp", axis=1, tiled=True),
+        prepare_shards_up(masters.astype(jnp.bfloat16)),
         lax.all_gather(level_table, "dp", axis=0, tiled=True),
     )
     w_qkv, w_out, w_up, w_down, w_mod = unpack(

time: 1300 us -> 1370 us (1.054)
  local copies, waits for them, and re-layouts: 168 us -> 224 us
    ppermute x0 -> x7, waiting for transfers between devices: none -> 101 us  [the longest x4 88 us: advance_the_cube(): far_arr = lax.ppermute(far_arr, perm=all_rows, axis_name=mesh_dim)]
    all_gather x1, waiting for transfers between devices: 59.1 us -> 0.01 us  [body(): lax.all_gather(masters.astype(jnp.bfloat16), 'dp', axis=1, tiled=True)]
    transpose x0 -> x5, local copies, waits for them, and re-layouts: none -> 14.5 us  [unpack(): matrices.append(stacked.transpose(0, 2, 1, 3).reshape(height, breadth))]
    gather x0 -> x1, local copies, waits for them, and re-layouts: none -> 14.1 us  [body(): jnp.take(regathered[0], inverse, axis=0)]
    unnamed x205 -> x221, local copies, waits for them, and re-layouts: 36.9 us -> 40.7 us
  transfers between devices with their start and end apart: 7 -> 14, of which waited for: 7 -> 10; matrix products, arithmetic and copies ran while one was open for 13% -> 16% of each run, Pallas kernels for 0% -> 0%
where the time goes in v1:
time: 1370 us; the launch traced here: 1360 us
  waiting for transfers between devices  767 us (56%)
  local copies, waits for them, and re-layouts  224 us (16%)
  matrix products  191 us (14%)
  other arithmetic  135 us (10%)
  blocking collectives  18.9 us (1%)
  between operations  15.8 us (1%)
    psum x1, waiting for transfers between devices, body(): lax.psum(jnp.dot(activated, w_down, preferred_element_type=jnp.float32).a...  231 us
    psum x1, waiting for transfers between devices, body(): lax.psum(jnp.dot(attended, w_out, preferred_element_type=jnp.float32).ast...  133 us
    psum x1, waiting for transfers between devices, body(): lax.psum(contract_cols(grad_pre, back_up).astype(jnp.bfloat16), 'mp')  130 us
    reduce_scatter x1, waiting for transfers between devices, body(): lax.psum_scatter(table_term, ('dp', 'mp'), scatter_dimension=0, tiled=True)  129 us
    ppermute x4, waiting for transfers between devices, advance_the_cube(): far_arr = lax.ppermute(far_arr, perm=all_rows, axis_name=mesh_dim)  88 us
    unnamed x221, local copies, waits for them, and re-layouts  40.7 us
    reduce_scatter x1, waiting for transfers between devices, body(): lax.psum_scatter(owned[None].astype(jnp.bfloat16), 'dp', scatter_dimensio...  40.4 us
    dot_general x5, matrix products, contract_cols(): lax.dot_general(left_side, right_side, (((1,), (1,)), ((), ())), preferre...  28.8 us
  transfers between devices with their start and end apart: 14, of which 10 were waited for; matrix products, arithmetic and copies ran while one was open for 16% of the time, Pallas kernels for 0%

profile of v1, /device:TPU:0, one launch (start us, length us, event | category | flops | bytes accessed | tf_op | source)
XLA Modules:
  0.0 1360.4 jit_solution(6008438301689442595)
XLA Ops:
  8.0 6.0 squeeze.43
  22.4 33.2 %collective-permute-done = bf16[1,36,128,128]{3,2,0,1:T(8,128)(2,1)} collective-permute-done((bf16[1,36,128,128]{3,2,0,1:T(8,128)(2,1)}, bf16[1,36,128,128]{3,2,0,1:T(8,128)(2,1)}, u32[]{:S(2)}, u32[]{:S(2)}) %collective-permute-start) | collective-permute-done | bytes 1179680 | tf_op jit(solution)/shard_map/ppermute | solution.py:35
  73.1 18.1 %collective-permute-done.2 = bf16[1,36,128,128]{3,2,0,1:T(8,128)(2,1)} collective-permute-done((bf16[1,36,128,128]{3,2,0,1:T(8,128)(2,1)}, bf16[1,36,128,128]{3,2,0,1:T(8,128)(2,1)}, u32[]{:S(2)}, u32[]{:S(2)}) %collective-permute-start.2) | collective-permute-done | bytes 1179680 | tf_op jit(solution)/shard_map/ppermute | solution.py:35
  94.3 13.3 collective-permute-done.3
  115.3 27.8 %collective-permute-done.4 = bf16[1,36,128,128]{3,2,0,1:T(8,128)(2,1)S(1)} collective-permute-done((bf16[1,36,128,128]{3,2,0,1:T(8,128)(2,1)}, bf16[1,36,128,128]{3,2,0,1:T(8,128)(2,1)S(1)}, u32[]{:S(2)}, u32[]{:S(2)}) %collective-permute-start.4) | collective-permute-done | bytes 1179680 | tf_op jit(solution)/shard_map/ppermute | solution.py:35
  152.1 8.9 collective-permute-done.6
  163.5 14.1 %gather_fusion.1 = bf16[288,128,128]{2,1,0:T(8,128)(2,1)} fusion(bf16[288,128,128]{2,1,0:T(8,128)(2,1)} %bitcast_dynamic-update-slice_fusion, s32[1024]{0:T(1024)} %pad_clamp_fusion.1), kind=kCustom, calls=%fused_computation.clone | custom fusion | bytes 18875520 | tf_op jit(solution)/shard_map/jit(_take)/gather | solution.py:209
  177.6 14.1 %gather_fusion.2 = bf16[288,128,128]{2,1,0:T(8,128)(2,1)} fusion(bf16[288,128,128]{2,1,0:T(8,128)(2,1)} %bitcast.464, s32[1024]{0:T(1024)S(1)} %copy-done.81), kind=kCustom, calls=%fused_computation.1.clone | custom fusion | bytes 18875520 | tf_op jit(solution)/shard_map/jit(_take)/gather | solution.py:298
  191.7 12.0 broadcast_select_fusion
  213.6 4.8 copy.204
  221.4 18.9 %all_gather.10 = f32[32,6144]{1,0:T(8,128)} all-gather(f32[32,1536]{1,0:T(8,128)S(1)} %fusion.69), channel_id=1, replica_groups=mesh['dp'=8,'mp'=4] {'mp'}, dimensions={1}, use_global_device_ids=true | all-gather | bytes 983040 | tf_op jit(solution)/shard_map/all_gather | solution.py:232
  258.6 4.7 reshape.538
  313.7 5.0 fusion.150
  329.0 6.1 convolution_convert_fusion.2
  335.1 132.9 %all-reduce.5.cloned.1.call-done = bf16[2048,1024]{1,0:T(8,128)(2,1)} async-done(((bf16[2048,1024]{1,0:T(8,128)(2,1)}), bf16[2048,1024]{1,0:T(8,128)(2,1)}) %all-reduce.5.cloned.1.call-update) | async-done | bytes 4194320 | tf_op jit(solution)/shard_map/psum | solution.py:271
  468.0 5.0 fusion.72
  478.6 15.2 %fusion.40 = (bf16[1024,2048]{1,0:T(8,128)(2,1)}, bf16[1024,2048]{1,0:T(8,128)(2,1)}, f32[2048,1024]{0,1:T(8,128)S(1)}) fusion(bf16[2048,1024]{0,1:T(8,128)(2,1)} %convolution_convert_fusion.2, bf16[2048,1024]{1,0:T(8,128)(2,1)S(1)} %fusion.35, bf16[128,8,8,128]{3,2,1,0:T(8,128)(2,1)S(1)} %bitcast.491), kind=kOutput, calls=%fused_computation.72 | convolution fusion | flops 4343201792 | bytes 27262976 | tf_op jit(solution)/shard_map/dot_general | solution.py:284
  497.2 12.7 fusion.63
  522.1 11.5 fusion.62
  533.6 130.4 %all-reduce.7.cloned.1.call-done = bf16[2048,1024]{1,0:T(8,128)(2,1)} async-done(((bf16[2048,1024]{1,0:T(8,128)(2,1)}), bf16[2048,1024]{1,0:T(8,128)(2,1)}) %all-reduce.7.cloned.1.call-update) | async-done | bytes 4194320 | tf_op jit(solution)/shard_map/psum | solution.py:308
  664.0 6.5 fusion.54
  672.3 8.4 fusion.28
  690.8 14.2 %multiply_reduce_fusion.1 = (f32[2,4,512]{2,1,0:T(4,128)S(1)}, f32[2,4,512,1024]{3,2,1,0:T(8,128)}) fusion(f32[2,4,512,1024]{3,2,1,0:T(8,128)} %copy-done.5, f32[2,4,512]{2,1,0:T(4,128)} %bitcast.510, bf16[2,512,4,64]{1,3,2,0:T(8,128)(2,1)} %copy.273, bf16[2,1024,4,64]{1,3,2,0:T(8,128)(2,1)} %copy.213), kind=kOutput, calls=%fused_computation.9 | convolution fusion | flops 549449728 | bytes 35160064 | tf_op jit(solution)/shard_map/cqhd,ckhd->chqk/dot_general | solution.py:156
  707.8 10.1 multiply_convert_fusion.1
  717.9 7.3 fusion.114
  729.5 7.6 fusion.36
  737.1 13.8 %multiply_reduce_fusion = (f32[2,4,512]{2,1,0:T(4,128)S(1)}, f32[2,4,512,1024]{3,2,1,0:T(8,128)}) fusion(f32[2,4,512,1024]{3,2,1,0:T(8,128)} %copy-done.4, f32[2,4,512]{2,1,0:T(4,128)S(1)} %bitcast.508, bf16[2,512,4,64]{1,3,2,0:T(8,128)(2,1)S(1)} %copy-done.32, bf16[2,1024,4,64]{1,3,2,0:T(8,128)(2,1)S(1)} %copy-done.22), kind=kOutput, calls=%fused_computation.6 | convolution fusion | flops 549449728 | bytes 35160064 | tf_op jit(solution)/shard_map/cqhd,ckhd->chqk/dot_general | solution.py:156
  750.9 9.1 fusion.106
  762.4 10.5 multiply_convert_fusion
  772.9 6.2 fusion.113
  785.6 5.6 convolution_convert_fusion.1
  793.8 6.5 copy.260
  800.3 6.5 copy.257
  808.1 6.5 copy.259
  814.6 8.7 fusion.162
  823.4 5.7 fusion.161
  830.4 6.5 copy.258
  837.0 6.4 fusion.159
  849.8 231.4 %all-reduce.9.cloned.1.call-done = (bf16[2048,1024]{1,0:T(8,128)(2,1)}, bf16[2048,1024]{1,0:T(8,128)(2,1)}) async-done(((bf16[2048,1024]{1,0:T(8,128)(2,1)}, bf16[2048,1024]{1,0:T(8,128)(2,1)}), (bf16[2048,1024]{1,0:T(8,128)(2,1)}, bf16[2048,1024]{1,0:T(8,128)(2,1)})) %all-reduce.9.cloned.1.call-update) | async-done | bytes 8388624 | tf_op jit(solution)/shard_map/psum | solution.py:287
  1081.2 17.0 %fusion.49 = (bf16[32,1024]{1,0:T(8,128)(2,1)S(1)}, bf16[32,1024]{1,0:T(8,128)(2,1)S(1)}, bf16[32,1024]{1,0:T(8,128)(2,1)S(1)}, bf16[32,1024]{1,0:T(8,128)(2,1)S...) fusion(bf16[2048,1024]{1,0:T(8,128)(2,1)} %all-reduce.7.cloned.1.call-done, ...), kind=kLoop, calls=%fused_computation.85 | loop fusion | flops 58523648 | bytes 25870336 | tf_op jit(solution)/shard_map/reduce_sum | solution.py:313
  1102.2 14.0 %gather_fusion = bf16[288,128,128]{2,1,0:T(8,128)(2,1)} fusion(bf16[288,128,128]{2,1,0:T(8,128)(2,1)} %constant_dynamic-update-slice_fusion.9, s32[1024]{0:T(1024)S(1)} %copy-done.82), kind=kCustom, calls=%fused_computation.2 | custom fusion | bytes 18875520 | tf_op jit(solution)/shard_map/jit(_take)/gather | solution.py:391
  1116.2 9.2 fusion
  1129.4 5.3 copy.237
  1142.7 5.9 fusion.43
  1148.7 12.3 fusion.46
  1161.0 40.4 %reduce-scatter.5.cloned.1.call-done = bf16[1,36,128,128]{3,2,1,0:T(8,128)(2,1)} async-done(((bf16[1,288,128,128]{3,2,1,0:T(8,128)(2,1)}), bf16[1,36,128,128]{3,2,1,0:T(8,128)(2,1)}) %reduce-scatter.5.cloned.1.call-update) | async-done | bytes 1179664 | tf_op jit(solution)/shard_map/reduce_scatter | solution.py:392
  1213.1 5.1 bitcast_subtract_fusion
  1223.7 129.5 %reduce-scatter.3.cloned.1.call-done = f32[32,1024]{1,0:T(8,128)} async-done(((f32[1024,1024]{1,0:T(8,128)}), f32[32,1024]{1,0:T(8,128)}) %reduce-scatter.3.cloned.1.call-update) | async-done | bytes 131088 | tf_op jit(solution)/shard_map/reduce_scatter | solution.py:389
  (364 shorter events, 233.9 us)
Async XLA Ops:
  7.2 1194.2 %copy-start = (f32[1,36,128,128]{3,2,1,0:T(8,128)S(1)}, f32[1,36,128,128]{3,2,1,0:T(8,128)}, u32[]{:S(2)}) copy-start(f32[1,36,128,128]{3,2,1,0:T(8,128)} %param.26) | copy-start | bytes 7077892
  7.2 12.3 copy-start.83
  7.2 12.3 copy-start.88
  7.2 12.8 copy-start.89
  7.2 12.8 copy-start.87
  7.2 142.1 %all-gather.3.cloned.1.call-start = ((), (), s32[]{:S(2)}) async-start(), calls=%async_computation.2 | async-start | bytes 2359296 | tf_op jit(solution)/shard_map/all_gather | solution.py:206
  8.0 169.6 %all-gather.5.cloned.1.call-start = ((), (), s32[]{:S(2)}) async-start(), calls=%async_computation.4 | async-start | bytes 10616832 | tf_op jit(solution)/shard_map/all_gather | solution.py:296
  14.0 48.8 %copy-start.79 = (s32[288]{0:T(512)S(1)}, s32[288]{0:T(512)}, u32[]{:S(2)}) copy-start(s32[288]{0:T(512)} %param.22) | copy-start | bytes 3460
  16.1 451.9 %all-reduce.5.cloned.1.call-start = ((), (), s32[]{:S(2)}) async-start(), calls=%async_computation.3 | async-start | bytes 8388608 | tf_op jit(solution)/shard_map/psum | solution.py:271
  16.1 51.5 %collective-permute-start.1 = (bf16[1,36,128,128]{3,2,0,1:T(8,128)(2,1)}, bf16[1,36,128,128]{3,2,0,1:T(8,128)(2,1)}, u32[]{:S(2)}, u32[]{:S(2)}) collective-permute-start(bf16[1,36,128,128]{3,2,0,1:T(8,128)(2,1)} %get-tuple-element.27), channel_id=1, source_target_pairs={{0,28},{4,0},{8,4},{12,8},{16,12},{20,16},{24,20},{28,24},{1,29},{... | collective-permute-start | bytes 3538952 | tf_op jit(solution)/shard_map/ppermute | solution.py:38
  19.5 36.1 %collective-permute-start = (bf16[1,36,128,128]{3,2,0,1:T(8,128)(2,1)}, bf16[1,36,128,128]{3,2,0,1:T(8,128)(2,1)}, u32[]{:S(2)}, u32[]{:S(2)}) collective-permute-start(bf16[1,36,128,128]{3,2,0,1:T(8,128)(2,1)} %get-tuple-element.27), channel_id=1, source_target_pairs={{0,4},{4,8},{8,12},{12,16},{16,20},{20,24},{24,28},{28,0},{1,5},{5... | collective-permute-start | bytes 3538952 | tf_op jit(solution)/shard_map/ppermute | solution.py:35
  55.6 35.7 %collective-permute-start.2 = (bf16[1,36,128,128]{3,2,0,1:T(8,128)(2,1)}, bf16[1,36,128,128]{3,2,0,1:T(8,128)(2,1)}, u32[]{:S(2)}, u32[]{:S(2)}) collective-permute-start(bf16[1,36,128,128]{3,2,0,1:T(8,128)(2,1)} %collective-permute-done), channel_id=1, source_target_pairs={{0,4},{4,8},{8,12},{12,16},{16,20},{20,24},{24,28},{28,0},{1,5},{5... | collective-permute-start | bytes 3538952 | tf_op jit(solution)/shard_map/ppermute | solution.py:35
  67.7 39.9 %collective-permute-start.3 = (bf16[1,36,128,128]{3,2,0,1:T(8,128)(2,1)}, bf16[1,36,128,128]{3,2,0,1:T(8,128)(2,1)S(1)}, u32[]{:S(2)}, u32[]{:S(2)}) collective-permute-start(bf16[1,36,128,128]{3,2,0,1:T(8,128)(2,1)} %collective-permute-done.1), channel_id=1, source_target_pairs={{0,28},{4,0},{8,4},{12,8},{16,12},{20,16},{24,20},{28,24},{1,29},{... | collective-permute-start | bytes 3538952 | tf_op jit(solution)/shard_map/ppermute | solution.py:38
  73.1 172.2 %copy-start.59 = (f32[2048]{0:T(1024)}, f32[2048]{0:T(1024)S(1)}, u32[]{:S(2)}) copy-start(f32[2048]{0:T(1024)S(1)} %broadcast_multiply_fusion.5) | copy-start | bytes 24580
  91.3 51.8 %collective-permute-start.4 = (bf16[1,36,128,128]{3,2,0,1:T(8,128)(2,1)}, bf16[1,36,128,128]{3,2,0,1:T(8,128)(2,1)S(1)}, u32[]{:S(2)}, u32[]{:S(2)}) collective-permute-start(bf16[1,36,128,128]{3,2,0,1:T(8,128)(2,1)} %collective-permute-done.2), channel_id=1, source_target_pairs={{0,4},{4,8},{8,12},{12,16},{16,20},{20,24},{24,28},{28,0},{1,5},{5... | collective-permute-start | bytes 3538952 | tf_op jit(solution)/shard_map/ppermute | solution.py:35
  94.3 151.0 %copy-start.65 = (f32[2048]{0:T(1024)}, f32[2048]{0:T(1024)S(1)}, u32[]{:S(2)}) copy-start(f32[2048]{0:T(1024)S(1)} %add_rsqrt_fusion.1) | copy-start | bytes 24580
  107.6 40.6 %collective-permute-start.5 = (bf16[1,36,128,128]{3,2,0,1:T(8,128)(2,1)S(1)}, bf16[1,36,128,128]{3,2,0,1:T(8,128)(2,1)S(1)}, u32[]{:S(2)}, u32[]{:S(2)}) collective-permute-start(bf16[1,36,128,128]{3,2,0,1:T(8,128)(2,1)S(1)} %collective-permute-done.3), channel_id=1, source_target_pairs={{0,28},{4,0},{8,4},{12,8},{16,12},{20,16},{24,20},{28,24},{1,29},{... | collective-permute-start | bytes 3538952 | tf_op jit(solution)/shard_map/ppermute | solution.py:38
  143.1 17.9 %collective-permute-start.6 = (bf16[1,36,128,128]{3,2,0,1:T(8,128)(2,1)S(1)}, bf16[1,36,128,128]{3,2,0,1:T(8,128)(2,1)}, u32[]{:S(2)}, u32[]{:S(2)}) collective-permute-start(bf16[1,36,128,128]{3,2,0,1:T(8,128)(2,1)S(1)} %collective-permute-done.4), channel_id=1, source_target_pairs={{0,4},{4,8},{8,12},{12,16},{16,20},{20,24},{24,28},{28,0},{1,5},{5... | collective-permute-start | bytes 3538952 | tf_op jit(solution)/shard_map/ppermute | solution.py:35
  163.5 14.1 %copy-start.81 = (s32[1024]{0:T(1024)S(1)}, s32[1024]{0:T(1024)}, u32[]{:S(2)}) copy-start(s32[1024]{0:T(1024)} %pad_clamp_fusion.1) | copy-start | bytes 12292
  177.6 14.1 %copy-start.86 = (pred[288]{0:T(512)(128)(4,1)S(1)}, pred[288]{0:T(512)(128)(4,1)}, u32[]{:S(2)}) copy-start(pred[288]{0:T(512)(128)(4,1)} %compare_and_fusion) | copy-start | bytes 868
  258.6 35.7 %copy-start.14 = (bf16[2,1024,4,64]{1,3,2,0:T(8,128)(2,1)}, bf16[2,1024,4,64]{1,3,2,0:T(8,128)(2,1)S(1)}, u32[]{:S(2)}) copy-start(bf16[2,1024,4,64]{1,3,2,0:T(8,128)(2,1)S(1)} %copy.212) | copy-start | bytes 3145732
  313.7 350.4 %all-reduce.7.cloned.1.call-start = ((), (), s32[]{:S(2)}) async-start(), calls=%async_computation.5 | async-start | bytes 8388608 | tf_op jit(solution)/shard_map/psum | solution.py:308
  478.6 15.3 %copy-start.19 = (bf16[2048,1024]{1,0:T(8,128)(2,1)}, bf16[2048,1024]{1,0:T(8,128)(2,1)S(1)}, u32[]{:S(2)}) copy-start(bf16[2048,1024]{1,0:T(8,128)(2,1)S(1)} %fusion.35) | copy-start | bytes 12582916
  478.6 18.6 %copy-start.45 = (bf16[8,8,128,128]{3,1,2,0:T(8,128)(2,1)S(1)}, bf16[8,8,128,128]{3,1,2,0:T(8,128)(2,1)}, u32[]{:S(2)}) copy-start(bf16[8,8,128,128]{3,1,2,0:T(8,128)(2,1)} %copy.223) | copy-start | bytes 6291460
  509.9 11.0 copy-start.68
  509.9 11.0 copy-start.78
  509.9 11.6 copy-start.70
  509.9 571.3 %all-reduce.9.cloned.1.call-start = ((), (), s32[]{:S(2)}) async-start(), calls=%async_computation.8 | async-start | bytes 16777216 | tf_op jit(solution)/shard_map/psum | solution.py:287
  690.8 14.2 %slice-start.4 = ((s8[16777216]{0:T(1024)(128)(4,1)}), s8[4194304]{0:T(1024)(128)(4,1)S(1)}, s32[]{:S(2)}) async-start(s8[16777216]{0:T(1024)(128)(4,1)} %bitcast.454), calls=%async_computation.13 | async-start | bytes 8388608
  690.8 14.2 %slice-start.5 = ((s8[16777216]{0:T(1024)(128)(4,1)}), s8[4194304]{0:T(1024)(128)(4,1)S(1)}, s32[]{:S(2)}) async-start(s8[16777216]{0:T(1024)(128)(4,1)} %bitcast.454), calls=%async_computation.14 | async-start | bytes 8388608
  690.8 15.7 %slice-start.6 = ((s8[16777216]{0:T(1024)(128)(4,1)}), s8[4194304]{0:T(1024)(128)(4,1)S(1)}, s32[]{:S(2)}) async-start(s8[16777216]{0:T(1024)(128)(4,1)} %bitcast.454), calls=%async_computation.15 | async-start | bytes 8388608
  690.8 16.9 %slice-start.7 = ((s8[16777216]{0:T(1024)(128)(4,1)}), s8[4194304]{0:T(1024)(128)(4,1)S(1)}, s32[]{:S(2)}) async-start(s8[16777216]{0:T(1024)(128)(4,1)} %bitcast.454), calls=%async_computation.16 | async-start | bytes 8388608
  690.8 16.9 %copy-start.62 = (f32[1,8,512]{2,1,0:T(8,128)S(1)}, f32[1,8,512]{2,1,0:T(8,128)}, u32[]{:S(2)}) copy-start(f32[1,8,512]{2,1,0:T(8,128)} %log_add_fusion.1) | copy-start | bytes 49156
  737.0 13.9 %copy-start.63 = (f32[1,8,512]{2,1,0:T(8,128)S(1)}, f32[1,8,512]{2,1,0:T(8,128)}, u32[]{:S(2)}) copy-start(f32[1,8,512]{2,1,0:T(8,128)} %log_add_fusion.1) | copy-start | bytes 49156
  737.1 25.3 %slice-start = ((s8[16777216]{0:T(1024)(128)(4,1)}), s8[4194304]{0:T(1024)(128)(4,1)S(1)}, s32[]{:S(2)}) async-start(s8[16777216]{0:T(1024)(128)(4,1)} %bitcast.452), calls=%async_computation.9 | async-start | bytes 8388608
  737.1 25.3 %slice-start.1 = ((s8[16777216]{0:T(1024)(128)(4,1)}), s8[4194304]{0:T(1024)(128)(4,1)S(1)}, s32[]{:S(2)}) async-start(s8[16777216]{0:T(1024)(128)(4,1)} %bitcast.452), calls=%async_computation.10 | async-start | bytes 8388608
  737.1 25.3 %slice-start.2 = ((s8[16777216]{0:T(1024)(128)(4,1)}), s8[4194304]{0:T(1024)(128)(4,1)S(1)}, s32[]{:S(2)}) async-start(s8[16777216]{0:T(1024)(128)(4,1)} %bitcast.452), calls=%async_computation.11 | async-start | bytes 8388608
  750.9 11.4 slice-start.3
  762.4 16.7 %copy-start.16 = (f32[2,4,64,1024]{3,2,1,0:T(8,128)S(1)}, f32[2,4,64,1024]{3,2,1,0:T(8,128)}, u32[]{:S(2)}) copy-start(f32[2,4,64,1024]{3,2,1,0:T(8,128)} %fusion.158) | copy-start | bytes 6291460
  791.2 410.2 %reduce-scatter.5.cloned.1.call-start = ((), (), s32[]{:S(2)}) async-start(), calls=%async_computation.7 | async-start | bytes 10616832 | tf_op jit(solution)/shard_map/reduce_scatter | solution.py:392
  844.7 236.5 %copy-start.39 = (f32[32,1024]{1,0:T(8,128)S(1)}, f32[32,1024]{1,0:T(8,128)}, u32[]{:S(2)}) copy-start(f32[32,1024]{1,0:T(8,128)} %get-tuple-element.47) | copy-start | bytes 393220
  844.7 236.5 %copy-start.75 = (f32[32,64]{1,0:T(8,128)S(1)}, f32[32,64]{1,0:T(8,128)}, u32[]{:S(2)}) copy-start(f32[32,64]{1,0:T(8,128)} %rsqrt.27) | copy-start | bytes 24580
  844.7 236.5 %copy-start.76 = (f32[32,64]{1,0:T(8,128)S(1)}, f32[32,64]{1,0:T(8,128)}, u32[]{:S(2)}) copy-start(f32[32,64]{1,0:T(8,128)} %div.65) | copy-start | bytes 24580
  1081.2 17.8 %copy-start.64 = (bf16[4,8,8,128]{3,2,1,0:T(8,128)(2,1)S(1)}, bf16[4,8,8,128]{3,2,1,0:T(8,128)(2,1)}, u32[]{:S(2)}) copy-start(bf16[4,8,8,128]{3,2,1,0:T(8,128)(2,1)} %copy.291) | copy-start | bytes 196612
  1102.2 14.0 %copy-start.85 = (pred[288]{0:T(512)(128)(4,1)S(1)}, pred[288]{0:T(512)(128)(4,1)}, u32[]{:S(2)}) copy-start(pred[288]{0:T(512)(128)(4,1)} %compare_and_fusion.1) | copy-start | bytes 868
  1125.4 12.5 copy-start.84
  1125.4 227.8 %reduce-scatter.3.cloned.1.call-start = ((), (), s32[]{:S(2)}) async-start(), calls=%async_computation.6 | async-start | bytes 4325376 | tf_op jit(solution)/shard_map/reduce_scatter | solution.py:389
  1129.4 13.3 copy-start.43
  (66 other events, 375.2 us)
Sparse Core Ops, SparseCore 0:
  9.9 38.9 all-gather.2
  51.4 90.7 all-gather.4
  313.8 154.1 all-reduce.4
  510.0 153.9 all-reduce.6
  791.3 289.8 all-reduce.8
  1125.5 75.7 reduce-scatter.4
  1204.2 148.9 reduce-scatter.2
